TPU v7x, 32 devices: a whole 2x2x4 slice. The times are simulated.
32 devices in a mesh: patch: 16 (over z, x, core), sec: 2 (over y).
Axes of the slice: x: 2, y: 2, z: 4, core: 2. Of those that a mesh axis runs over, the one named last changes fastest.
Arguments:
- concentration: float32 [16, 8, 128, 128], P('patch', 'sec'), may hold values from -1 to 1
- partner: int32 [16, 4], replicated, may hold values from 0 to 15, as said below
- face_id: int32 [16, 4], replicated, may hold values from 0 to 3, as said below
- flip: int32 [16, 4], replicated, may hold values from 0 to 1, as said below
Outputs:
- evolved: float32 [16, 8, 128, 128], P('patch', 'sec')
Inputs may be any that keep to these rules, and one draw needn't show every extreme that they name: Across face f of patch p lies face face_id[p, f] of patch partner[p, f], and across that face lies face f of patch p again; the four partners of a patch are four different patches, none of them p itself. `face_id`: see partner. `flip`: equal on the two sides of an interface.
All inputs are finite; a program needn't handle non-finite values.
Results may differ from a plain program's by a relative error of at most 0.0001.
Values sent between devices are 32-bit elements; how exact they have to be, the bound alone decides.
No kernel may reach another device: no remote copies, remote signals or barrier semaphores. Data moves between devices by JAX's collectives and lax.ppermute only.
A program may use at most 64 MiB of HBM per device.

v0:
```python
import jax
import jax.numpy as jnp
from jax import lax
from jax.sharding import PartitionSpec as P

ITERS = 3
STEPS = 2
MASS_BAND = (2416.0 / 5040.0, 1191.0 / 5040.0, 120.0 / 5040.0, 1.0 / 5040.0)
STIFF_BAND = (2.0 / 3.0, -0.125, -0.2, -1.0 / 120.0)
PENALTY = 2.0
TIME_STEP = 1.0
STABILIZER = 2.0
GRADIENT_ENERGY = 0.5


def padded_2(cells, sides, width):
    for axis, dim in sides:
        count = lax.axis_size(axis)
        ends = count - 1
        head = lax.slice_in_dim(cells, 0, width, axis=dim)
        tail = lax.slice_in_dim(cells, cells.shape[dim] - width, cells.shape[dim], axis=dim)
        cells = jnp.concatenate(
            [
                lax.ppermute(tail, axis, [(i, (i + 1) % count) for i in range(ends)]),
                cells,
                lax.ppermute(head, axis, [((i + 1) % count, i) for i in range(ends)]),
            ],
            axis=dim,
        )
    return cells


def banded_padded(padded, coefficients, along, length):
    summed = coefficients[0] * lax.slice_in_dim(padded, 3, 3 + length, axis=along)
    for offset in range(1, 4):
        lower = lax.slice_in_dim(padded, 3 - offset, 3 - offset + length, axis=along)
        upper = lax.slice_in_dim(padded, 3 + offset, 3 + offset + length, axis=along)
        summed = summed + coefficients[offset] * (lower + upper)
    return summed


def banded(field, coefficients, along):
    length = field.shape[along]
    widths = [(0, 0)] * field.ndim
    widths[along] = (3, 3)
    return banded_padded(jnp.pad(field, widths), coefficients, along, length)


def tensor_parts(mass_third, stiff_third, first_axis, second_axis):
    mass_both = banded(mass_third, MASS_BAND, second_axis)
    stiff_second = banded(mass_third, STIFF_BAND, second_axis)
    mixed_second = banded(stiff_third, MASS_BAND, second_axis)
    stiffness = banded(mass_both, STIFF_BAND, first_axis) + banded(
        stiff_second + mixed_second, MASS_BAND, first_axis
    )
    return (mass_both, stiffness)


def face_traces(field):
    return jnp.stack(
        [field[..., 0, :], field[..., -1, :], field[..., :, 0], field[..., :, -1]],
        axis=field.ndim - 3,
    )


def add_penalty(stiffness, mismatch, face_axis):
    pieces = [lax.index_in_dim(mismatch, number, face_axis, keepdims=False) for number in range(4)]
    stiffness = stiffness.at[..., 0, :].add(PENALTY * pieces[0])
    stiffness = stiffness.at[..., -1, :].add(PENALTY * pieces[1])
    stiffness = stiffness.at[..., :, 0].add(PENALTY * pieces[2])
    stiffness = stiffness.at[..., :, -1].add(PENALTY * pieces[3])
    return stiffness


def partner_traces(traces, partner_row, face_row, flip_row):
    all_traces = lax.all_gather(traces[None], "patch", axis=0, tiled=True)
    picked = all_traces[partner_row, face_row]
    return jnp.where(flip_row[:, None, None] == 1, picked[..., ::-1], picked)


def stiffness_local(field, tables, with_mass):
    length = field.shape[0]
    padded = padded_2(field, (("sec", 0),), 3)
    mass_third = banded_padded(padded, MASS_BAND, 0, length)
    stiff_third = banded_padded(padded, STIFF_BAND, 0, length)
    mass_both, stiffness = tensor_parts(mass_third, stiff_third, 1, 2)
    traces = face_traces(field)
    others = partner_traces(traces, tables[0], tables[1], tables[2])
    stiffness = add_penalty(stiffness, traces - others, 0)
    mass_full = banded(mass_both, MASS_BAND, 1) if with_mass else None
    return (mass_full, stiffness)


def operate(direction, tables):
    mass_full, stiff_one = stiffness_local(direction, tables, True)
    unused, stiff_two = stiffness_local(stiff_one, tables, False)
    return mass_full + TIME_STEP * STABILIZER * stiff_one + TIME_STEP * GRADIENT_ENERGY * stiff_two


def squares(residual):
    return lax.psum(jnp.sum(residual * residual), ("patch", "sec"))


def shards(concentration, partner, face_id, flip):
    patch_now = lax.axis_index("patch")
    tables = (
        lax.dynamic_index_in_dim(partner, patch_now, 0, keepdims=False),
        lax.dynamic_index_in_dim(face_id, patch_now, 0, keepdims=False),
        lax.dynamic_index_in_dim(flip, patch_now, 0, keepdims=False),
    )
    iterate = concentration[0]
    for section in range(STEPS):
        current = iterate
        unused, curvature = stiffness_local(current, tables, False)
        potential = current * current * current - current + GRADIENT_ENERGY * curvature
        unused, flux = stiffness_local(potential, tables, False)
        residual = -TIME_STEP * flux
        direction = residual
        norm_now = squares(residual)
        for iteration in range(ITERS):
            image = operate(direction, tables)
            step_size = norm_now / lax.psum(jnp.sum(direction * image), ("patch", "sec"))
            iterate = iterate + step_size * direction
            if iteration + 1 < ITERS:
                residual = residual - step_size * image
                norm_next = squares(residual)
                direction = residual + norm_next / norm_now * direction
                norm_now = norm_next
    return iterate[None]


def solution(mesh):
    placed = (P("patch", "sec", None, None), P(), P(), P())
    return jax.shard_map(
        shards, mesh=mesh, in_specs=placed, out_specs=P("patch", "sec", None, None), check_vma=False
    )
```

profile of v0, /device:TPU:14, one launch (start us, length us, event | category | flops | bytes accessed | tf_op | source)
XLA Modules:
  0.0 1101.7 jit_solution(2193271219574866490)
XLA Ops:
  1.2 2.4 collective-permute-start.1
  5.3 15.5 %all-gather = f32[64,4,128]{2,1,0:T(4,128)S(1)} all-gather(f32[4,4,128]{2,1,0:T(4,128)S(1)} %pad_maximum_fusion.32), channel_id=2, replica_groups=mesh['patch'=16,'sec'=2] {'patch'}, dimensions={0}, use_global_device_ids=true | all-gather | bytes 139264 | tf_op jit(solution)/shard_map/all_gather | solution.py:76
  27.0 2.2 scatter-add.214
  29.4 10.8 scatter-add.215
  41.1 4.6 collective-permute-start.3
  46.9 21.8 %all-gather.1 = f32[64,4,128]{2,1,0:T(4,128)S(1)} all-gather(f32[4,4,128]{2,1,0:T(4,128)S(1)} %pad_maximum_fusion.33), channel_id=3, replica_groups=mesh['patch'=16,'sec'=2] {'patch'}, dimensions={0}, use_global_device_ids=true | all-gather | bytes 139264 | tf_op jit(solution)/shard_map/all_gather | solution.py:76
  70.8 2.5 multiply_add_fusion.54
  74.5 4.6 collective-permute-start.5
  80.6 17.5 %all-gather.2 = f32[64,4,128]{2,1,0:T(4,128)S(1)} all-gather(f32[4,4,128]{2,1,0:T(4,128)S(1)} %pad_maximum_fusion.34), channel_id=4, replica_groups=mesh['patch'=16,'sec'=2] {'patch'}, dimensions={0}, use_global_device_ids=true | all-gather | bytes 139264 | tf_op jit(solution)/shard_map/all_gather | solution.py:76
  105.2 10.8 scatter-add.229
  116.3 4.6 collective-permute-start.7
  122.4 19.8 %all-gather.3 = f32[64,4,128]{2,1,0:T(4,128)S(1)} all-gather(f32[4,4,128]{2,1,0:T(4,128)S(1)} %pad_maximum_fusion.35), channel_id=5, replica_groups=mesh['patch'=16,'sec'=2] {'patch'}, dimensions={0}, use_global_device_ids=true | all-gather | bytes 139264 | tf_op jit(solution)/shard_map/all_gather | solution.py:76
  149.1 10.8 scatter-add.235
  161.5 44.3 %all-reduce.65 = (f32[]{:T(128)}, f32[]{:T(128)}) all-reduce(f32[]{:T(128)} %get-tuple-element.776, f32[]{:T(128)} %get-tuple-element.775), channel_id=1, replica_groups=mesh['patch'=16,'sec'=2] {'patch','sec'}, use_global_device_ids=true, to_apply=%region_1.2 | all-reduce | flops 2 | bytes 16 | tf_op jit(solution)/shard_map/psum | solution.py:101
  207.8 38.7 %psum.86 = f32[]{:T(128)} all-reduce(f32[]{:T(128)} %get-tuple-element.825), channel_id=1, replica_groups=mesh['patch'=16,'sec'=2] {'patch','sec'}, use_global_device_ids=true, to_apply=%region_5.6 | all-reduce | flops 1 | bytes 8 | tf_op jit(solution)/shard_map/psum | solution.py:101
  248.2 3.4 collective-permute-start.9
  253.1 16.2 %all-gather.4 = f32[64,4,128]{2,1,0:T(4,128)S(1)} all-gather(f32[4,4,128]{2,1,0:T(4,128)S(1)} %pad_maximum_fusion.36), channel_id=6, replica_groups=mesh['patch'=16,'sec'=2] {'patch'}, dimensions={0}, use_global_device_ids=true | all-gather | bytes 139264 | tf_op jit(solution)/shard_map/all_gather | solution.py:76
  276.1 10.8 scatter-add.241
  287.9 4.6 collective-permute-start.11
  294.1 20.9 %all-gather.5 = f32[64,4,128]{2,1,0:T(4,128)S(1)} all-gather(f32[4,4,128]{2,1,0:T(4,128)S(1)} %pad_maximum_fusion.37), channel_id=7, replica_groups=mesh['patch'=16,'sec'=2] {'patch'}, dimensions={0}, use_global_device_ids=true | all-gather | bytes 139264 | tf_op jit(solution)/shard_map/all_gather | solution.py:76
  319.5 2.2 scatter-add.246
  321.8 10.8 scatter-add.249
  334.1 44.3 %psum.87 = f32[]{:T(128)} all-reduce(f32[]{:T(128)} %get-tuple-element.817), channel_id=1, replica_groups=mesh['patch'=16,'sec'=2] {'patch','sec'}, use_global_device_ids=true, to_apply=%region_7.8 | all-reduce | flops 1 | bytes 8 | tf_op jit(solution)/shard_map/psum | solution.py:122
  380.4 38.6 %psum.88 = f32[]{:T(128)} all-reduce(f32[]{:T(128)} %multiply_reduce_fusion.7), channel_id=1, replica_groups=mesh['patch'=16,'sec'=2] {'patch','sec'}, use_global_device_ids=true, to_apply=%region_9.10 | all-reduce | flops 1 | bytes 8 | tf_op jit(solution)/shard_map/psum | solution.py:101
  420.7 3.4 collective-permute-start.13
  425.6 16.3 %all-gather.6 = f32[64,4,128]{2,1,0:T(4,128)S(1)} all-gather(f32[4,4,128]{2,1,0:T(4,128)S(1)} %pad_maximum_fusion.38), channel_id=8, replica_groups=mesh['patch'=16,'sec'=2] {'patch'}, dimensions={0}, use_global_device_ids=true | all-gather | bytes 139264 | tf_op jit(solution)/shard_map/all_gather | solution.py:76
  448.8 10.8 scatter-add.255
  460.6 4.6 collective-permute-start.15
  466.7 21.2 %all-gather.7 = f32[64,4,128]{2,1,0:T(4,128)S(1)} all-gather(f32[4,4,128]{2,1,0:T(4,128)S(1)} %pad_maximum_fusion.39), channel_id=9, replica_groups=mesh['patch'=16,'sec'=2] {'patch'}, dimensions={0}, use_global_device_ids=true | all-gather | bytes 139264 | tf_op jit(solution)/shard_map/all_gather | solution.py:76
  492.4 2.2 scatter-add.260
  494.7 10.8 scatter-add.261
  507.0 44.3 %psum.89 = f32[]{:T(128)} all-reduce(f32[]{:T(128)} %multiply_reduce_fusion.6), channel_id=1, replica_groups=mesh['patch'=16,'sec'=2] {'patch','sec'}, use_global_device_ids=true, to_apply=%region_11.12 | all-reduce | flops 1 | bytes 8 | tf_op jit(solution)/shard_map/psum | solution.py:122
  556.7 13.8 %all-gather.8 = f32[64,4,128]{2,1,0:T(4,128)S(1)} all-gather(f32[4,4,128]{2,1,0:T(4,128)S(1)} %pad_maximum_fusion.40), channel_id=10, replica_groups=mesh['patch'=16,'sec'=2] {'patch'}, dimensions={0}, use_global_device_ids=true | all-gather | bytes 139264 | tf_op jit(solution)/shard_map/all_gather | solution.py:76
  577.3 10.8 scatter-add.269
  588.5 4.6 collective-permute-start.19
  594.6 21.2 %all-gather.9 = f32[64,4,128]{2,1,0:T(4,128)S(1)} all-gather(f32[4,4,128]{2,1,0:T(4,128)S(1)} %pad_maximum_fusion.41), channel_id=11, replica_groups=mesh['patch'=16,'sec'=2] {'patch'}, dimensions={0}, use_global_device_ids=true | all-gather | bytes 139264 | tf_op jit(solution)/shard_map/all_gather | solution.py:76
  622.7 10.8 scatter-add.275
  634.2 4.6 collective-permute-start.21
  640.3 17.7 %all-gather.10 = f32[64,4,128]{2,1,0:T(4,128)S(1)} all-gather(f32[4,4,128]{2,1,0:T(4,128)S(1)} %pad_maximum_fusion.42), channel_id=12, replica_groups=mesh['patch'=16,'sec'=2] {'patch'}, dimensions={0}, use_global_device_ids=true | all-gather | bytes 139264 | tf_op jit(solution)/shard_map/all_gather | solution.py:76
  660.8 2.5 multiply_add_fusion.21
  665.8 10.8 scatter-add.281
  677.8 4.6 collective-permute-start.23
  683.9 19.9 %all-gather.11 = f32[64,4,128]{2,1,0:T(4,128)S(1)} all-gather(f32[4,4,128]{2,1,0:T(4,128)S(1)} %pad_maximum_fusion.43), channel_id=13, replica_groups=mesh['patch'=16,'sec'=2] {'patch'}, dimensions={0}, use_global_device_ids=true | all-gather | bytes 139264 | tf_op jit(solution)/shard_map/all_gather | solution.py:76
  710.8 10.8 scatter-add.289
  722.7 44.4 %all-reduce.64 = (f32[]{:T(128)}, f32[]{:T(128)}) all-reduce(f32[]{:T(128)} %get-tuple-element.774, f32[]{:T(128)} %get-tuple-element.773), channel_id=1, replica_groups=mesh['patch'=16,'sec'=2] {'patch','sec'}, use_global_device_ids=true, to_apply=%region_13.14 | all-reduce | flops 2 | bytes 16 | tf_op jit(solution)/shard_map/psum | solution.py:101
  769.4 38.6 %psum.92 = f32[]{:T(128)} all-reduce(f32[]{:T(128)} %get-tuple-element.797), channel_id=1, replica_groups=mesh['patch'=16,'sec'=2] {'patch','sec'}, use_global_device_ids=true, to_apply=%region_17.18 | all-reduce | flops 1 | bytes 8 | tf_op jit(solution)/shard_map/psum | solution.py:101
  809.6 3.4 collective-permute-start.25
  814.3 16.2 %all-gather.12 = f32[64,4,128]{2,1,0:T(4,128)S(1)} all-gather(f32[4,4,128]{2,1,0:T(4,128)S(1)} %pad_maximum_fusion.44), channel_id=14, replica_groups=mesh['patch'=16,'sec'=2] {'patch'}, dimensions={0}, use_global_device_ids=true | all-gather | bytes 139264 | tf_op jit(solution)/shard_map/all_gather | solution.py:76
  832.6 2.5 multiply_add_fusion.14
  838.3 10.8 scatter-add.299
  849.1 4.6 collective-permute-start.27
  855.1 20.9 %all-gather.13 = f32[64,4,128]{2,1,0:T(4,128)S(1)} all-gather(f32[4,4,128]{2,1,0:T(4,128)S(1)} %pad_maximum_fusion.45), channel_id=15, replica_groups=mesh['patch'=16,'sec'=2] {'patch'}, dimensions={0}, use_global_device_ids=true | all-gather | bytes 139264 | tf_op jit(solution)/shard_map/all_gather | solution.py:76
  878.7 2.5 multiply_add_fusion.10
  884.0 10.8 scatter-add.305
  895.7 44.2 %psum.93 = f32[]{:T(128)} all-reduce(f32[]{:T(128)} %multiply_reduce_fusion.2), channel_id=1, replica_groups=mesh['patch'=16,'sec'=2] {'patch','sec'}, use_global_device_ids=true, to_apply=%region_19.20 | all-reduce | flops 1 | bytes 8 | tf_op jit(solution)/shard_map/psum | solution.py:122
  942.0 38.6 %psum.94 = f32[]{:T(128)} all-reduce(f32[]{:T(128)} %get-tuple-element.789), channel_id=1, replica_groups=mesh['patch'=16,'sec'=2] {'patch','sec'}, use_global_device_ids=true, to_apply=%region_21.22 | all-reduce | flops 1 | bytes 8 | tf_op jit(solution)/shard_map/psum | solution.py:101
  982.3 3.4 collective-permute-start.29
  987.0 16.3 %all-gather.14 = f32[64,4,128]{2,1,0:T(4,128)S(1)} all-gather(f32[4,4,128]{2,1,0:T(4,128)S(1)} %pad_maximum_fusion.46), channel_id=16, replica_groups=mesh['patch'=16,'sec'=2] {'patch'}, dimensions={0}, use_global_device_ids=true | all-gather | bytes 139264 | tf_op jit(solution)/shard_map/all_gather | solution.py:76
  1005.3 2.5 multiply_add_fusion.5
  1010.9 10.8 scatter-add.311
  1021.8 4.6 collective-permute-start.31
  1027.8 20.7 %all-gather.15 = f32[64,4,128]{2,1,0:T(4,128)S(1)} all-gather(f32[4,4,128]{2,1,0:T(4,128)S(1)} %pad_maximum_fusion.47), channel_id=17, replica_groups=mesh['patch'=16,'sec'=2] {'patch'}, dimensions={0}, use_global_device_ids=true | all-gather | bytes 139264 | tf_op jit(solution)/shard_map/all_gather | solution.py:76
  1050.8 2.5 multiply_add_fusion.1
  1054.7 44.3 %psum.95 = f32[]{:T(128)} all-reduce(f32[]{:T(128)} %multiply_reduce_fusion), channel_id=1, replica_groups=mesh['patch'=16,'sec'=2] {'patch','sec'}, use_global_device_ids=true, to_apply=%region_23.24 | all-reduce | flops 1 | bytes 8 | tf_op jit(solution)/shard_map/psum | solution.py:122
  (425 shorter events, 136.0 us)
Async XLA Ops:
  1.1 3.9 copy-start
  1.2 22.4 %collective-permute-start.1 = (f32[3,128,128]{1,0,2:T(4,128)S(1)}, f32[3,128,128]{1,0,2:T(4,128)S(1)}, u32[]{:S(2)}, u32[]{:S(2)}) collective-permute-start(f32[3,128,128]{1,0,2:T(4,128)S(1)} %get-tuple-element.957), channel_id=1, source_target_pairs={{1,0},{3,2},{5,4},{7,6},{9,8},{11,10},{13,12},{15,14},{17,16},{19,... | collective-permute-start | bytes 589832 | tf_op jit(solution)/shard_map/ppermute | solution.py:26
  3.7 20.0 %collective-permute-start = (f32[3,128,128]{1,0,2:T(4,128)S(1)}, f32[3,128,128]{1,0,2:T(4,128)S(1)}, u32[]{:S(2)}, u32[]{:S(2)}) collective-permute-start(f32[3,128,128]{1,0,2:T(4,128)S(1)} %get-tuple-element.956), channel_id=1, source_target_pairs={{0,1},{2,3},{4,5},{6,7},{8,9},{10,11},{12,13},{14,15},{16,17},{18,... | collective-permute-start | bytes 589832 | tf_op jit(solution)/shard_map/ppermute | solution.py:24
  20.8 0.7 copy-start.3
  20.8 0.7 copy-start.2
  22.3 0.7 copy-start.1
  41.1 28.7 %collective-permute-start.3 = (f32[3,128,128]{2,0,1:T(4,128)S(1)}, f32[3,128,128]{2,0,1:T(4,128)S(1)}, u32[]{:S(2)}, u32[]{:S(2)}) collective-permute-start(f32[3,128,128]{2,0,1:T(4,128)S(1)} %get-tuple-element.949), channel_id=1, source_target_pairs={{1,0},{3,2},{5,4},{7,6},{9,8},{11,10},{13,12},{15,14},{17,16},{19,... | collective-permute-start | bytes 589832 | tf_op jit(solution)/shard_map/ppermute | solution.py:26
  45.6 24.1 %collective-permute-start.2 = (f32[3,128,128]{2,0,1:T(4,128)S(1)}, f32[3,128,128]{2,0,1:T(4,128)S(1)}, u32[]{:S(2)}, u32[]{:S(2)}) collective-permute-start(f32[3,128,128]{2,0,1:T(4,128)S(1)} %get-tuple-element.948), channel_id=1, source_target_pairs={{0,1},{2,3},{4,5},{6,7},{8,9},{10,11},{12,13},{14,15},{16,17},{18,... | collective-permute-start | bytes 589832 | tf_op jit(solution)/shard_map/ppermute | solution.py:24
  74.5 24.4 %collective-permute-start.5 = (f32[3,128,128]{1,0,2:T(4,128)S(1)}, f32[3,128,128]{1,0,2:T(4,128)S(1)}, u32[]{:S(2)}, u32[]{:S(2)}) collective-permute-start(f32[3,128,128]{1,0,2:T(4,128)S(1)} %get-tuple-element.945), channel_id=1, source_target_pairs={{1,0},{3,2},{5,4},{7,6},{9,8},{11,10},{13,12},{15,14},{17,16},{19,... | collective-permute-start | bytes 589832 | tf_op jit(solution)/shard_map/ppermute | solution.py:26
  79.1 19.8 %collective-permute-start.4 = (f32[3,128,128]{1,0,2:T(4,128)S(1)}, f32[3,128,128]{1,0,2:T(4,128)S(1)}, u32[]{:S(2)}, u32[]{:S(2)}) collective-permute-start(f32[3,128,128]{1,0,2:T(4,128)S(1)} %get-tuple-element.944), channel_id=1, source_target_pairs={{0,1},{2,3},{4,5},{6,7},{8,9},{10,11},{12,13},{14,15},{16,17},{18,... | collective-permute-start | bytes 589832 | tf_op jit(solution)/shard_map/ppermute | solution.py:24
  116.3 27.1 %collective-permute-start.7 = (f32[3,128,128]{1,0,2:T(4,128)S(1)}, f32[3,128,128]{1,0,2:T(4,128)S(1)}, u32[]{:S(2)}, u32[]{:S(2)}) collective-permute-start(f32[3,128,128]{1,0,2:T(4,128)S(1)} %get-tuple-element.937), channel_id=1, source_target_pairs={{1,0},{3,2},{5,4},{7,6},{9,8},{11,10},{13,12},{15,14},{17,16},{19,... | collective-permute-start | bytes 589832 | tf_op jit(solution)/shard_map/ppermute | solution.py:26
  120.9 22.5 %collective-permute-start.6 = (f32[3,128,128]{1,0,2:T(4,128)S(1)}, f32[3,128,128]{1,0,2:T(4,128)S(1)}, u32[]{:S(2)}, u32[]{:S(2)}) collective-permute-start(f32[3,128,128]{1,0,2:T(4,128)S(1)} %get-tuple-element.936), channel_id=1, source_target_pairs={{0,1},{2,3},{4,5},{6,7},{8,9},{10,11},{12,13},{14,15},{16,17},{18,... | collective-permute-start | bytes 589832 | tf_op jit(solution)/shard_map/ppermute | solution.py:24
  248.2 22.2 %collective-permute-start.9 = (f32[3,128,128]{1,0,2:T(4,128)S(1)}, f32[3,128,128]{1,0,2:T(4,128)S(1)}, u32[]{:S(2)}, u32[]{:S(2)}) collective-permute-start(f32[3,128,128]{1,0,2:T(4,128)S(1)} %get-tuple-element.931), channel_id=1, source_target_pairs={{1,0},{3,2},{5,4},{7,6},{9,8},{11,10},{13,12},{15,14},{17,16},{19,... | collective-permute-start | bytes 589832 | tf_op jit(solution)/shard_map/ppermute | solution.py:26
  251.5 18.9 %collective-permute-start.8 = (f32[3,128,128]{1,0,2:T(4,128)S(1)}, f32[3,128,128]{1,0,2:T(4,128)S(1)}, u32[]{:S(2)}, u32[]{:S(2)}) collective-permute-start(f32[3,128,128]{1,0,2:T(4,128)S(1)} %get-tuple-element.930), channel_id=1, source_target_pairs={{0,1},{2,3},{4,5},{6,7},{8,9},{10,11},{12,13},{14,15},{16,17},{18,... | collective-permute-start | bytes 589832 | tf_op jit(solution)/shard_map/ppermute | solution.py:24
  287.9 28.2 %collective-permute-start.11 = (f32[3,128,128]{1,0,2:T(4,128)}, f32[3,128,128]{1,0,2:T(4,128)S(1)}, u32[]{:S(2)}, u32[]{:S(2)}) collective-permute-start(f32[3,128,128]{1,0,2:T(4,128)} %get-tuple-element.923), channel_id=1, source_target_pairs={{1,0},{3,2},{5,4},{7,6},{9,8},{11,10},{13,12},{15,14},{17,16},{19,... | collective-permute-start | bytes 589832 | tf_op jit(solution)/shard_map/ppermute | solution.py:26
  292.5 23.6 %collective-permute-start.10 = (f32[3,128,128]{1,0,2:T(4,128)S(1)}, f32[3,128,128]{1,0,2:T(4,128)S(1)}, u32[]{:S(2)}, u32[]{:S(2)}) collective-permute-start(f32[3,128,128]{1,0,2:T(4,128)S(1)} %get-tuple-element.922), channel_id=1, source_target_pairs={{0,1},{2,3},{4,5},{6,7},{8,9},{10,11},{12,13},{14,15},{16,17},{18,... | collective-permute-start | bytes 589832 | tf_op jit(solution)/shard_map/ppermute | solution.py:24
  420.7 22.4 %collective-permute-start.13 = (f32[3,128,128]{1,0,2:T(4,128)S(1)}, f32[3,128,128]{1,0,2:T(4,128)S(1)}, u32[]{:S(2)}, u32[]{:S(2)}) collective-permute-start(f32[3,128,128]{1,0,2:T(4,128)S(1)} %get-tuple-element.917), channel_id=1, source_target_pairs={{1,0},{3,2},{5,4},{7,6},{9,8},{11,10},{13,12},{15,14},{17,16},{19,... | collective-permute-start | bytes 589832 | tf_op jit(solution)/shard_map/ppermute | solution.py:26
  424.1 19.0 %collective-permute-start.12 = (f32[3,128,128]{1,0,2:T(4,128)S(1)}, f32[3,128,128]{1,0,2:T(4,128)S(1)}, u32[]{:S(2)}, u32[]{:S(2)}) collective-permute-start(f32[3,128,128]{1,0,2:T(4,128)S(1)} %get-tuple-element.916), channel_id=1, source_target_pairs={{0,1},{2,3},{4,5},{6,7},{8,9},{10,11},{12,13},{14,15},{16,17},{18,... | collective-permute-start | bytes 589832 | tf_op jit(solution)/shard_map/ppermute | solution.py:24
  460.6 28.4 %collective-permute-start.15 = (f32[3,128,128]{1,0,2:T(4,128)}, f32[3,128,128]{1,0,2:T(4,128)S(1)}, u32[]{:S(2)}, u32[]{:S(2)}) collective-permute-start(f32[3,128,128]{1,0,2:T(4,128)} %get-tuple-element.909), channel_id=1, source_target_pairs={{1,0},{3,2},{5,4},{7,6},{9,8},{11,10},{13,12},{15,14},{17,16},{19,... | collective-permute-start | bytes 589832 | tf_op jit(solution)/shard_map/ppermute | solution.py:26
  465.2 23.8 %collective-permute-start.14 = (f32[3,128,128]{1,0,2:T(4,128)S(1)}, f32[3,128,128]{1,0,2:T(4,128)S(1)}, u32[]{:S(2)}, u32[]{:S(2)}) collective-permute-start(f32[3,128,128]{1,0,2:T(4,128)S(1)} %get-tuple-element.908), channel_id=1, source_target_pairs={{0,1},{2,3},{4,5},{6,7},{8,9},{10,11},{12,13},{14,15},{16,17},{18,... | collective-permute-start | bytes 589832 | tf_op jit(solution)/shard_map/ppermute | solution.py:24
  553.1 18.5 %collective-permute-start.17 = (f32[3,128,128]{1,0,2:T(4,128)S(1)}, f32[3,128,128]{1,0,2:T(4,128)S(1)}, u32[]{:S(2)}, u32[]{:S(2)}) collective-permute-start(f32[3,128,128]{1,0,2:T(4,128)S(1)} %get-tuple-element.903), channel_id=1, source_target_pairs={{1,0},{3,2},{5,4},{7,6},{9,8},{11,10},{13,12},{15,14},{17,16},{19,... | collective-permute-start | bytes 589832 | tf_op jit(solution)/shard_map/ppermute | solution.py:26
  555.1 16.5 %collective-permute-start.16 = (f32[3,128,128]{1,0,2:T(4,128)S(1)}, f32[3,128,128]{1,0,2:T(4,128)S(1)}, u32[]{:S(2)}, u32[]{:S(2)}) collective-permute-start(f32[3,128,128]{1,0,2:T(4,128)S(1)} %get-tuple-element.902), channel_id=1, source_target_pairs={{0,1},{2,3},{4,5},{6,7},{8,9},{10,11},{12,13},{14,15},{16,17},{18,... | collective-permute-start | bytes 589832 | tf_op jit(solution)/shard_map/ppermute | solution.py:24
  588.5 28.5 %collective-permute-start.19 = (f32[3,128,128]{1,0,2:T(4,128)S(1)}, f32[3,128,128]{1,0,2:T(4,128)S(1)}, u32[]{:S(2)}, u32[]{:S(2)}) collective-permute-start(f32[3,128,128]{1,0,2:T(4,128)S(1)} %get-tuple-element.895), channel_id=1, source_target_pairs={{1,0},{3,2},{5,4},{7,6},{9,8},{11,10},{13,12},{15,14},{17,16},{19,... | collective-permute-start | bytes 589832 | tf_op jit(solution)/shard_map/ppermute | solution.py:26
  593.1 23.9 %collective-permute-start.18 = (f32[3,128,128]{1,0,2:T(4,128)S(1)}, f32[3,128,128]{1,0,2:T(4,128)S(1)}, u32[]{:S(2)}, u32[]{:S(2)}) collective-permute-start(f32[3,128,128]{1,0,2:T(4,128)S(1)} %get-tuple-element.894), channel_id=1, source_target_pairs={{0,1},{2,3},{4,5},{6,7},{8,9},{10,11},{12,13},{14,15},{16,17},{18,... | collective-permute-start | bytes 589832 | tf_op jit(solution)/shard_map/ppermute | solution.py:24
  634.2 25.0 %collective-permute-start.21 = (f32[3,128,128]{1,0,2:T(4,128)S(1)}, f32[3,128,128]{1,0,2:T(4,128)S(1)}, u32[]{:S(2)}, u32[]{:S(2)}) collective-permute-start(f32[3,128,128]{1,0,2:T(4,128)S(1)} %get-tuple-element.887), channel_id=1, source_target_pairs={{1,0},{3,2},{5,4},{7,6},{9,8},{11,10},{13,12},{15,14},{17,16},{19,... | collective-permute-start | bytes 589832 | tf_op jit(solution)/shard_map/ppermute | solution.py:26
  638.8 20.4 %collective-permute-start.20 = (f32[3,128,128]{1,0,2:T(4,128)S(1)}, f32[3,128,128]{1,0,2:T(4,128)S(1)}, u32[]{:S(2)}, u32[]{:S(2)}) collective-permute-start(f32[3,128,128]{1,0,2:T(4,128)S(1)} %get-tuple-element.886), channel_id=1, source_target_pairs={{0,1},{2,3},{4,5},{6,7},{8,9},{10,11},{12,13},{14,15},{16,17},{18,... | collective-permute-start | bytes 589832 | tf_op jit(solution)/shard_map/ppermute | solution.py:24
  677.8 27.3 %collective-permute-start.23 = (f32[3,128,128]{1,0,2:T(4,128)}, f32[3,128,128]{1,0,2:T(4,128)S(1)}, u32[]{:S(2)}, u32[]{:S(2)}) collective-permute-start(f32[3,128,128]{1,0,2:T(4,128)} %get-tuple-element.879), channel_id=1, source_target_pairs={{1,0},{3,2},{5,4},{7,6},{9,8},{11,10},{13,12},{15,14},{17,16},{19,... | collective-permute-start | bytes 589832 | tf_op jit(solution)/shard_map/ppermute | solution.py:26
  682.3 22.7 %collective-permute-start.22 = (f32[3,128,128]{1,0,2:T(4,128)S(1)}, f32[3,128,128]{1,0,2:T(4,128)S(1)}, u32[]{:S(2)}, u32[]{:S(2)}) collective-permute-start(f32[3,128,128]{1,0,2:T(4,128)S(1)} %get-tuple-element.878), channel_id=1, source_target_pairs={{0,1},{2,3},{4,5},{6,7},{8,9},{10,11},{12,13},{14,15},{16,17},{18,... | collective-permute-start | bytes 589832 | tf_op jit(solution)/shard_map/ppermute | solution.py:24
  809.6 21.9 %collective-permute-start.25 = (f32[3,128,128]{2,0,1:T(4,128)S(1)}, f32[3,128,128]{2,0,1:T(4,128)S(1)}, u32[]{:S(2)}, u32[]{:S(2)}) collective-permute-start(f32[3,128,128]{2,0,1:T(4,128)S(1)} %get-tuple-element.871), channel_id=1, source_target_pairs={{1,0},{3,2},{5,4},{7,6},{9,8},{11,10},{13,12},{15,14},{17,16},{19,... | collective-permute-start | bytes 589832 | tf_op jit(solution)/shard_map/ppermute | solution.py:26
  813.0 18.5 %collective-permute-start.24 = (f32[3,128,128]{2,0,1:T(4,128)S(1)}, f32[3,128,128]{2,0,1:T(4,128)S(1)}, u32[]{:S(2)}, u32[]{:S(2)}) collective-permute-start(f32[3,128,128]{2,0,1:T(4,128)S(1)} %get-tuple-element.870), channel_id=1, source_target_pairs={{0,1},{2,3},{4,5},{6,7},{8,9},{10,11},{12,13},{14,15},{16,17},{18,... | collective-permute-start | bytes 589832 | tf_op jit(solution)/shard_map/ppermute | solution.py:24
  849.1 28.0 %collective-permute-start.27 = (f32[3,128,128]{2,0,1:T(4,128)S(1)}, f32[3,128,128]{2,0,1:T(4,128)S(1)}, u32[]{:S(2)}, u32[]{:S(2)}) collective-permute-start(f32[3,128,128]{2,0,1:T(4,128)S(1)} %get-tuple-element.863), channel_id=1, source_target_pairs={{1,0},{3,2},{5,4},{7,6},{9,8},{11,10},{13,12},{15,14},{17,16},{19,... | collective-permute-start | bytes 589832 | tf_op jit(solution)/shard_map/ppermute | solution.py:26
  853.7 23.5 %collective-permute-start.26 = (f32[3,128,128]{2,0,1:T(4,128)S(1)}, f32[3,128,128]{2,0,1:T(4,128)S(1)}, u32[]{:S(2)}, u32[]{:S(2)}) collective-permute-start(f32[3,128,128]{2,0,1:T(4,128)S(1)} %get-tuple-element.862), channel_id=1, source_target_pairs={{0,1},{2,3},{4,5},{6,7},{8,9},{10,11},{12,13},{14,15},{16,17},{18,... | collective-permute-start | bytes 589832 | tf_op jit(solution)/shard_map/ppermute | solution.py:24
  982.3 21.9 %collective-permute-start.29 = (f32[3,128,128]{2,0,1:T(4,128)S(1)}, f32[3,128,128]{2,0,1:T(4,128)S(1)}, u32[]{:S(2)}, u32[]{:S(2)}) collective-permute-start(f32[3,128,128]{2,0,1:T(4,128)S(1)} %get-tuple-element.855), channel_id=1, source_target_pairs={{1,0},{3,2},{5,4},{7,6},{9,8},{11,10},{13,12},{15,14},{17,16},{19,... | collective-permute-start | bytes 589832 | tf_op jit(solution)/shard_map/ppermute | solution.py:26
  985.6 18.6 %collective-permute-start.28 = (f32[3,128,128]{2,0,1:T(4,128)S(1)}, f32[3,128,128]{2,0,1:T(4,128)S(1)}, u32[]{:S(2)}, u32[]{:S(2)}) collective-permute-start(f32[3,128,128]{2,0,1:T(4,128)S(1)} %get-tuple-element.854), channel_id=1, source_target_pairs={{0,1},{2,3},{4,5},{6,7},{8,9},{10,11},{12,13},{14,15},{16,17},{18,... | collective-permute-start | bytes 589832 | tf_op jit(solution)/shard_map/ppermute | solution.py:24
  1021.8 27.5 %collective-permute-start.31 = (f32[3,128,128]{2,0,1:T(4,128)S(1)}, f32[3,128,128]{2,0,1:T(4,128)S(1)}, u32[]{:S(2)}, u32[]{:S(2)}) collective-permute-start(f32[3,128,128]{2,0,1:T(4,128)S(1)} %get-tuple-element.847), channel_id=1, source_target_pairs={{1,0},{3,2},{5,4},{7,6},{9,8},{11,10},{13,12},{15,14},{17,16},{19,... | collective-permute-start | bytes 589832 | tf_op jit(solution)/shard_map/ppermute | solution.py:26
  1026.4 22.9 %collective-permute-start.30 = (f32[3,128,128]{2,0,1:T(4,128)S(1)}, f32[3,128,128]{2,0,1:T(4,128)S(1)}, u32[]{:S(2)}, u32[]{:S(2)}) collective-permute-start(f32[3,128,128]{2,0,1:T(4,128)S(1)} %get-tuple-element.846), channel_id=1, source_target_pairs={{0,1},{2,3},{4,5},{6,7},{8,9},{10,11},{12,13},{14,15},{16,17},{18,... | collective-permute-start | bytes 589832 | tf_op jit(solution)/shard_map/ppermute | solution.py:24
where the time goes:
time: 1110 us; the launch traced here: 1100 us
  blocking collectives  716 us (65%)
  local copies, waits for them, and re-layouts  212 us (19%)
  starting transfers between devices  84.4 us (8%)
  other arithmetic  72.7 us (7%)
  between operations  15.9 us (1%)
    all_gather x16, blocking collectives, partner_traces(): all_traces = lax.all_gather(traces[None], 'patch', axis=0, tiled=True)  296 us
    psum x6, blocking collectives, squares(): return lax.psum(jnp.sum(residual * residual), ('patch', 'sec'))  243 us
    psum x4, blocking collectives, shards(): lax.psum(jnp.sum(direction * image), ('patch', 'sec'))  177 us
    scatter-add x13, local copies, waits for them, and re-layouts, add_penalty(): stiffness = stiffness.at[..., -1, :].add(PENALTY * pieces[1])  119 us
    ppermute x16, starting transfers between devices, padded_2(): lax.ppermute(head, axis, [((i + 1) % count, i) for i in range(ends)])  63.7 us
    add x42, other arithmetic, banded_padded(): summed = summed + coefficients[offset] * (lower + upper)  34.7 us
    scatter-add x10, local copies, waits for them, and re-layouts, add_penalty(): stiffness = stiffness.at[..., :, -1].add(PENALTY * pieces[3])  32.8 us
    scatter-add x11, local copies, waits for them, and re-layouts, add_penalty(): stiffness = stiffness.at[..., 0, :].add(PENALTY * pieces[0])  23.7 us
  transfers between devices with their start and end apart: 32, of which 0 were waited for; matrix products, arithmetic and copies ran while one was open for 2% of the time, Pallas kernels for 0%

commit v1 on v0

--- a/solution.py
+++ b/solution.py
@@ -73,7 +73,14 @@
 
 
 def partner_traces(traces, partner_row, face_row, flip_row):
-    all_traces = lax.all_gather(traces[None], "patch", axis=0, tiled=True)
+    block = traces[None]
+    devices = lax.axis_size("patch")
+    held, parts = (block, [block])
+    for _ in range(devices - 1):
+        held = lax.ppermute(held, "patch", [(i_2, (i_2 + 1) % devices) for i_2 in range(devices)])
+        parts.insert(0, held)
+    merged = jnp.concatenate(parts, axis=0)
+    all_traces = jnp.roll(merged, (lax.axis_index("patch") + 1) * block.shape[0], axis=0)
     picked = all_traces[partner_row, face_row]
     return jnp.where(flip_row[:, None, None] == 1, picked[..., ::-1], picked)
 

time: 1110 us -> 2180 us (1.96)
  waiting for transfers between devices: 0.08 us -> 1020 us
  starting transfers between devices: 84.4 us -> 258 us
  blocking collectives: 716 us -> 556 us
  local copies, waits for them, and re-layouts: 212 us -> 244 us
    ppermute x0 -> x240, waiting for transfers between devices: none -> 974 us  [partner_traces(): lax.ppermute(held, 'patch', [(i_2, (i_2 + 1) % devices) for i_2 in range(...]
    all_gather x16 -> x0, blocking collectives: 296 us -> none  [partner_traces(): all_traces = lax.all_gather(traces[None], 'patch', axis=0, tiled=True)]
    ppermute x0 -> x240, starting transfers between devices: none -> 160 us  [partner_traces(): lax.ppermute(held, 'patch', [(i_2, (i_2 + 1) % devices) for i_2 in range(...]
    psum x4, blocking collectives: 177 us -> 263 us  [shards(): lax.psum(jnp.sum(direction * image), ('patch', 'sec'))]
    psum x6, blocking collectives: 243 us -> 293 us  [squares(): return lax.psum(jnp.sum(residual * residual), ('patch', 'sec'))]
    scatter-add x13 -> x16, local copies, waits for them, and re-layouts: 119 us -> 161 us  [add_penalty(): stiffness = stiffness.at[..., -1, :].add(PENALTY * pieces[1])]
    scatter-add x10 -> x7, local copies, waits for them, and re-layouts: 32.8 us -> 11 us  [add_penalty(): stiffness = stiffness.at[..., :, -1].add(PENALTY * pieces[3])]
  transfers between devices with their start and end apart: 32 -> 272, of which waited for: 0 -> 254; matrix products, arithmetic and copies ran while one was open for 2% -> 1% of each run, Pallas kernels for 0% -> 0%
where the time goes in v1:
time: 2180 us; the launch traced here: 2160 us
  waiting for transfers between devices  1020 us (47%)
  blocking collectives  556 us (26%)
  starting transfers between devices  258 us (12%)
  local copies, waits for them, and re-layouts  244 us (11%)
  other arithmetic  73.8 us (3%)
    ppermute x240, waiting for transfers between devices, partner_traces(): lax.ppermute(held, 'patch', [(i_2, (i_2 + 1) % devices) for i_2 in range(...  974 us
    psum x6, blocking collectives, squares(): return lax.psum(jnp.sum(residual * residual), ('patch', 'sec'))  293 us
    psum x4, blocking collectives, shards(): lax.psum(jnp.sum(direction * image), ('patch', 'sec'))  263 us
    scatter-add x16, local copies, waits for them, and re-layouts, add_penalty(): stiffness = stiffness.at[..., -1, :].add(PENALTY * pieces[1])  161 us
    ppermute x240, starting transfers between devices, partner_traces(): lax.ppermute(held, 'patch', [(i_2, (i_2 + 1) % devices) for i_2 in range(...  160 us
    ppermute x16, starting transfers between devices, padded_2(): lax.ppermute(head, axis, [((i + 1) % count, i) for i in range(ends)])  77.1 us
  transfers between devices with their start and end apart: 272, of which 254 were waited for; matrix products, arithmetic and copies ran while one was open for 1% of the time, Pallas kernels for 0%

profile of v1, /device:TPU:14, one launch (start us, length us, event | category | flops | bytes accessed | tf_op | source)
XLA Modules:
  0.0 2164.5 jit_solution(17049075802559992741)
XLA Ops:
  70.0 10.8 scatter-add.215
  81.5 6.2 collective-permute-done.19
  92.9 6.3 collective-permute-done.21
  104.5 6.3 collective-permute-done.23
  122.4 5.8 collective-permute-done.26
  128.1 5.8 collective-permute-done.27
  133.9 5.8 collective-permute-done.28
  139.7 5.8 collective-permute-done.29
  145.5 5.8 collective-permute-done.30
  151.2 5.8 collective-permute-done.31
  178.3 10.8 scatter-add.221
  194.4 6.9 collective-permute-done.37
  205.9 6.9 collective-permute-done.39
  217.4 6.9 collective-permute-done.41
  230.1 5.8 collective-permute-done.43
  235.9 5.8 collective-permute-done.44
  286.7 10.8 scatter-add.229
  302.8 6.8 collective-permute-done.54
  314.3 6.8 collective-permute-done.56
  325.9 6.8 collective-permute-done.58
  394.4 10.8 scatter-add.235
  406.7 65.8 %all-reduce.65 = (f32[]{:T(128)}, f32[]{:T(128)}) all-reduce(f32[]{:T(128)} %get-tuple-element.777, f32[]{:T(128)} %get-tuple-element.776), channel_id=1, replica_groups=mesh['patch'=16,'sec'=2] {'patch','sec'}, use_global_device_ids=true, to_apply=%region_1.3 | all-reduce | flops 2 | bytes 16 | tf_op jit(solution)/shard_map/psum | solution.py:108
  474.6 40.3 %psum.86 = f32[]{:T(128)} all-reduce(f32[]{:T(128)} %get-tuple-element.832), channel_id=1, replica_groups=mesh['patch'=16,'sec'=2] {'patch','sec'}, use_global_device_ids=true, to_apply=%region_5.7 | all-reduce | flops 1 | bytes 8 | tf_op jit(solution)/shard_map/psum | solution.py:108
  590.3 10.8 scatter-add.241
  604.7 6.6 collective-permute-done.88
  616.0 6.9 collective-permute-done.90
  627.5 6.9 collective-permute-done.92
  696.2 10.8 scatter-add.249
  708.5 65.7 %psum.87 = f32[]{:T(128)} all-reduce(f32[]{:T(128)} %get-tuple-element.824), channel_id=1, replica_groups=mesh['patch'=16,'sec'=2] {'patch','sec'}, use_global_device_ids=true, to_apply=%region_7.9 | all-reduce | flops 1 | bytes 8 | tf_op jit(solution)/shard_map/psum | solution.py:129
  776.4 40.4 %psum.88 = f32[]{:T(128)} all-reduce(f32[]{:T(128)} %multiply_reduce_fusion.7), channel_id=1, replica_groups=mesh['patch'=16,'sec'=2] {'patch','sec'}, use_global_device_ids=true, to_apply=%region_9.11 | all-reduce | flops 1 | bytes 8 | tf_op jit(solution)/shard_map/psum | solution.py:108
  892.3 10.8 scatter-add.255
  906.7 6.6 collective-permute-done.122
  918.0 6.9 collective-permute-done.124
  929.5 6.9 collective-permute-done.126
  998.1 10.8 scatter-add.261
  1010.4 65.7 %psum.89 = f32[]{:T(128)} all-reduce(f32[]{:T(128)} %multiply_reduce_fusion.6), channel_id=1, replica_groups=mesh['patch'=16,'sec'=2] {'patch','sec'}, use_global_device_ids=true, to_apply=%region_11.13 | all-reduce | flops 1 | bytes 8 | tf_op jit(solution)/shard_map/psum | solution.py:129
  1150.6 10.8 scatter-add.269
  1166.0 6.3 collective-permute-done.156
  1176.9 6.9 collective-permute-done.158
  1188.5 6.9 collective-permute-done.160
  1257.1 10.8 scatter-add.275
  1273.3 6.8 collective-permute-done.173
  1284.8 6.8 collective-permute-done.175
  1296.3 6.8 collective-permute-done.177
  1364.9 10.8 scatter-add.281
  1381.0 6.8 collective-permute-done.190
  1392.5 6.8 collective-permute-done.192
  1404.1 6.8 collective-permute-done.194
  1472.6 10.8 scatter-add.289
  1485.0 65.8 %all-reduce.64 = (f32[]{:T(128)}, f32[]{:T(128)}) all-reduce(f32[]{:T(128)} %get-tuple-element.775, f32[]{:T(128)} %get-tuple-element.774), channel_id=1, replica_groups=mesh['patch'=16,'sec'=2] {'patch','sec'}, use_global_device_ids=true, to_apply=%region_13.15 | all-reduce | flops 2 | bytes 16 | tf_op jit(solution)/shard_map/psum | solution.py:108
  1552.8 40.3 %psum.92 = f32[]{:T(128)} all-reduce(f32[]{:T(128)} %get-tuple-element.803), channel_id=1, replica_groups=mesh['patch'=16,'sec'=2] {'patch','sec'}, use_global_device_ids=true, to_apply=%region_17.19 | all-reduce | flops 1 | bytes 8 | tf_op jit(solution)/shard_map/psum | solution.py:108
  1668.6 10.8 scatter-add.295
  1683.0 6.6 collective-permute-done.224
  1694.2 6.9 collective-permute-done.226
  1705.7 6.9 collective-permute-done.228
  1774.4 10.8 scatter-add.301
  1786.7 65.7 %psum.93 = f32[]{:T(128)} all-reduce(f32[]{:T(128)} %get-tuple-element.795), channel_id=1, replica_groups=mesh['patch'=16,'sec'=2] {'patch','sec'}, use_global_device_ids=true, to_apply=%region_19.21 | all-reduce | flops 1 | bytes 8 | tf_op jit(solution)/shard_map/psum | solution.py:129
  1854.6 40.3 %psum.94 = f32[]{:T(128)} all-reduce(f32[]{:T(128)} %multiply_reduce_fusion.1), channel_id=1, replica_groups=mesh['patch'=16,'sec'=2] {'patch','sec'}, use_global_device_ids=true, to_apply=%region_21.23 | all-reduce | flops 1 | bytes 8 | tf_op jit(solution)/shard_map/psum | solution.py:108
  1970.5 10.8 scatter-add.309
  1981.6 10.8 scatter-add.311
  1995.6 6.6 collective-permute-done.258
  2006.8 6.9 collective-permute-done.260
  2018.4 6.9 collective-permute-done.262
  2096.1 65.7 %psum.95 = f32[]{:T(128)} all-reduce(f32[]{:T(128)} %multiply_reduce_fusion), channel_id=1, replica_groups=mesh['patch'=16,'sec'=2] {'patch','sec'}, use_global_device_ids=true, to_apply=%region_23.25 | all-reduce | flops 1 | bytes 8 | tf_op jit(solution)/shard_map/psum | solution.py:129
  (1184 shorter events, 1171.2 us)
Async XLA Ops:
  50.7 7.9 collective-permute-start.15
  51.7 12.5 collective-permute-start
  53.0 11.2 collective-permute-start.1
  162.9 8.3 collective-permute-start.17
  164.2 8.4 collective-permute-start.18
  194.3 6.9 collective-permute-start.37
  205.9 6.9 collective-permute-start.39
  217.4 6.9 collective-permute-start.41
  270.5 6.4 collective-permute-start.50
  270.6 8.3 collective-permute-start.34
  271.9 8.4 collective-permute-start.35
  302.8 6.8 collective-permute-start.54
  314.3 6.8 collective-permute-start.56
  325.9 6.8 collective-permute-start.58
  378.9 8.3 collective-permute-start.51
  380.2 8.4 collective-permute-start.52
  573.0 10.4 collective-permute-start.68
  574.3 10.3 collective-permute-start.69
  604.7 6.6 collective-permute-start.88
  616.0 6.9 collective-permute-start.90
  627.5 6.9 collective-permute-start.92
  680.6 6.4 collective-permute-start.101
  680.7 8.3 collective-permute-start.85
  682.0 8.4 collective-permute-start.86
  875.0 10.4 collective-permute-start.102
  876.3 10.3 collective-permute-start.103
  906.7 6.6 collective-permute-start.122
  917.9 6.9 collective-permute-start.124
  929.5 6.9 collective-permute-start.126
  982.7 8.3 collective-permute-start.119
  984.0 8.4 collective-permute-start.120
  1133.9 9.3 collective-permute-start.136
  1135.2 9.7 collective-permute-start.137
  1165.4 6.9 collective-permute-start.156
  1176.9 6.9 collective-permute-start.158
  1188.5 6.9 collective-permute-start.160
  1241.6 6.5 collective-permute-start.169
  1241.7 8.3 collective-permute-start.153
  1243.0 8.4 collective-permute-start.154
  1273.2 6.8 collective-permute-start.173
  1284.8 6.8 collective-permute-start.175
  1296.3 6.8 collective-permute-start.177
  1349.4 8.3 collective-permute-start.170
  1350.7 8.4 collective-permute-start.171
  1381.0 6.8 collective-permute-start.190
  1392.5 6.8 collective-permute-start.192
  1404.1 6.8 collective-permute-start.194
  1457.2 8.3 collective-permute-start.187
  1458.5 8.4 collective-permute-start.188
  1651.1 6.4 collective-permute-start.220
  1651.2 10.4 collective-permute-start.204
  1652.5 10.3 collective-permute-start.205
  1683.0 6.6 collective-permute-start.224
  1694.2 6.9 collective-permute-start.226
  1705.7 6.9 collective-permute-start.228
  1758.9 8.3 collective-permute-start.221
  1760.2 8.4 collective-permute-start.222
  1953.1 10.4 collective-permute-start.238
  1954.4 10.3 collective-permute-start.239
  1995.6 6.6 collective-permute-start.258
  2006.8 6.9 collective-permute-start.260
  2018.4 6.9 collective-permute-start.262
  2071.6 8.3 collective-permute-start.255
  2072.9 8.4 collective-permute-start.256
  (219 other events, 1029.3 us)
